TPU v7x, 256 devices: a whole 4x4x8 slice. The times are simulated.
256 devices in a mesh: dp: 4 (over x), row: 8 (over z_lo, core), col: 8 (over z_hi, y).
Axes of the slice: x: 4, y: 4, z: 8 (z_hi: 2, z_lo: 4; z = z_hi * 4 + z_lo), core: 2. Of those that a mesh axis runs over, the one named last changes fastest.
Arguments:
- tokens: bfloat16 [4096, 8192], P(('dp', 'col'), 'row'), may hold values from -6 to 6
- gate_weight: bfloat16 [8192, 14336], P('row', ('dp', 'col')), may hold values from -0.0625 to 0.0625
- up_weight: bfloat16 [8192, 14336], P('row', ('dp', 'col')), may hold values from -0.0625 to 0.0625
- down_weight: bfloat16 [14336, 8192], P(('dp', 'col'), 'row'), may hold values from -0.046875 to 0.046875
Outputs:
- mixed: bfloat16 [4096, 8192], P(('dp', 'col'), 'row')
All inputs are finite; a program needn't handle non-finite values.
Results may differ from a plain program's by a relative error of at most 0.03.
Values may be sent and summed in bfloat16 or wider, within the bound.
A program may use at most 64 MiB of HBM per device.

v0:
```python
import jax
import jax.numpy as jnp
from jax import lax
from jax.sharding import PartitionSpec as P


def on_device(tokens, gate_weight, up_weight, down_weight):
    group_tokens = lax.all_gather(tokens, "col", axis=0, tiled=True)
    gate_cols, up_cols = (
        lax.all_gather(gate_weight, "dp", axis=1, tiled=True),
        lax.all_gather(up_weight, "dp", axis=1, tiled=True),
    )
    gate_term = jnp.dot(group_tokens, gate_cols, preferred_element_type=jnp.float32)
    up_term = jnp.dot(group_tokens, up_cols, preferred_element_type=jnp.float32)
    row_sums = lax.psum_scatter(
        jnp.concatenate((gate_term, up_term), axis=1).astype(jnp.bfloat16),
        "row",
        scatter_dimension=0,
        tiled=True,
    ).astype(jnp.float32)
    half_width = gate_cols.shape[1]
    gate_sum = row_sums[:, :half_width]
    up_sum = row_sums[:, half_width:]
    hidden = (jax.nn.silu(gate_sum) * up_sum).astype(jnp.bfloat16)
    hidden_all = lax.all_gather(hidden, "row", axis=0, tiled=True)
    down_term = jnp.dot(
        hidden_all,
        lax.all_gather(down_weight, "dp", axis=0, tiled=True),
        preferred_element_type=jnp.float32,
    )
    mixed = lax.psum_scatter(down_term.astype(jnp.bfloat16), "col", scatter_dimension=0, tiled=True)
    return mixed


def solution(mesh):
    return jax.shard_map(
        on_device,
        mesh=mesh,
        in_specs=(
            P(("dp", "col"), "row"),
            P("row", ("dp", "col")),
            P("row", ("dp", "col")),
            P(("dp", "col"), "row"),
        ),
        out_specs=P(("dp", "col"), "row"),
        check_vma=False,
    )
```

profile of v0, /device:TPU:2, one launch (start us, length us, event | category | flops | bytes accessed | tf_op | source)
XLA Modules:
  0.0 489.1 jit_solution(3508342044773073556)
XLA Ops:
  6.5 0.0 all-gather.6.cloned.1.call-start
  6.5 0.7 all-gather.6.cloned.1.call-update
  7.3 0.0 all-gather.8.cloned.1.call-start
  7.3 0.7 all-gather.8.cloned.1.call-update
  8.0 0.0 all-gather.10.cloned.1.call-start
  8.1 0.7 all-gather.10.cloned.1.call-update
  8.7 0.0 reduce-scatter.3.cloned.1.call-start
  8.8 80.1 %all-gather.6.cloned.1.call-done = bf16[1024,1024]{1,0:T(8,128)(2,1)} async-done(((bf16[128,1024]{1,0:T(8,128)(2,1)}), bf16[1024,1024]{1,0:T(8,128)(2,1)}) %all-gather.6.cloned.1.call-update) | async-done | bytes 2097168 | tf_op jit(solution)/shard_map/all_gather | solution.py:8
  88.9 43.2 %all-gather.8.cloned.1.call-done = bf16[1024,1792]{0,1:T(8,128)(2,1)} async-done(((bf16[1024,448]{0,1:T(8,128)(2,1)}), bf16[1024,1792]{0,1:T(8,128)(2,1)}) %all-gather.8.cloned.1.call-update) | async-done | bytes 3670032 | tf_op jit(solution)/shard_map/all_gather | solution.py:10
  132.1 8.5 %convolution_convert_fusion.1 = bf16[1024,1792]{1,0:T(8,128)(2,1)} fusion(bf16[1024,1024]{1,0:T(8,128)(2,1)} %all-gather.6.cloned.1.call-done, bf16[1024,1792]{0,1:T(8,128)(2,1)} %all-gather.8.cloned.1.call-done), kind=kOutput, calls=%fused_computation.2 | convolution fusion | flops 3759931392 | bytes 9437184 | tf_op jit(solution)/shard_map/dot_general | solution.py:13
  140.6 40.0 %all-gather.10.cloned.1.call-done = bf16[1024,1792]{0,1:T(8,128)(2,1)} async-done(((bf16[1024,448]{0,1:T(8,128)(2,1)}), bf16[1024,1792]{0,1:T(8,128)(2,1)}) %all-gather.10.cloned.1.call-update) | async-done | bytes 3670032 | tf_op jit(solution)/shard_map/all_gather | solution.py:11
  180.6 0.0 copy-start
  180.6 8.7 %convolution_convert_fusion = bf16[1024,1792]{1,0:T(8,128)(2,1)} fusion(bf16[1024,1024]{1,0:T(8,128)(2,1)} %all-gather.6.cloned.1.call-done, bf16[1024,1792]{0,1:T(8,128)(2,1)} %all-gather.10.cloned.1.call-done), kind=kOutput, calls=%fused_computation.1 | convolution fusion | flops 3759931392 | bytes 9437184 | tf_op jit(solution)/shard_map/dot_general | solution.py:14
  189.3 0.0 copy-done
  189.3 5.5 %pad_maximum_fusion = bf16[1024,3584]{1,0:T(8,128)(2,1)} fusion(bf16[1024,1792]{1,0:T(8,128)(2,1)} %convolution_convert_fusion, bf16[1024,1792]{1,0:T(8,128)(2,1)S(1)} %copy-done), kind=kLoop, calls=%fused_computation | loop fusion | flops 14680064 | bytes 14680064 | tf_op jit(solution)/shard_map/concatenate | solution.py:16
  194.8 0.0 reduce-scatter.3.cloned.1.call-update
  194.9 0.0 all-gather.14.cloned.1.call-start
  194.9 0.5 all-gather.14.cloned.1.call-update
  195.5 0.0 all-gather.12.cloned.1.call-start
  195.5 85.4 %reduce-scatter.3.cloned.1.call-done = bf16[128,3584]{1,0:T(8,128)(2,1)} async-done(((bf16[1024,3584]{1,0:T(8,128)(2,1)}), bf16[128,3584]{1,0:T(8,128)(2,1)}) %reduce-scatter.3.cloned.1.call-update) | async-done | bytes 917520 | tf_op jit(solution)/shard_map/reduce_scatter | solution.py:15
  280.9 1.4 convert_element_type.10
  282.3 1.0 fusion
  283.3 0.0 all-gather.12.cloned.1.call-update
  283.3 0.0 reduce-scatter.5.cloned.1.call-start
  283.4 43.5 %all-gather.14.cloned.1.call-done = bf16[1792,1024]{1,0:T(8,128)(2,1)} async-done(((bf16[448,1024]{1,0:T(8,128)(2,1)}), bf16[1792,1024]{1,0:T(8,128)(2,1)}) %all-gather.14.cloned.1.call-update) | async-done | bytes 3670032 | tf_op jit(solution)/shard_map/all_gather | solution.py:28
  326.9 52.3 %all-gather.12.cloned.1.call-done = bf16[1024,1792]{1,0:T(8,128)(2,1)} async-done(((bf16[128,1792]{1,0:T(8,128)(2,1)}), bf16[1024,1792]{1,0:T(8,128)(2,1)}) %all-gather.12.cloned.1.call-update) | async-done | bytes 3670032 | tf_op jit(solution)/shard_map/all_gather | solution.py:25
  379.2 8.4 %convolution_convert_fusion.2 = bf16[1024,1024]{1,0:T(8,128)(2,1)} fusion(bf16[1024,1792]{1,0:T(8,128)(2,1)} %all-gather.12.cloned.1.call-done, bf16[1792,1024]{1,0:T(8,128)(2,1)} %all-gather.14.cloned.1.call-done), kind=kOutput, calls=%fused_computation.3 | convolution fusion | flops 3759144960 | bytes 9437184 | tf_op jit(solution)/shard_map/dot_general | solution.py:26
  387.6 0.0 reduce-scatter.5.cloned.1.call-update
  387.6 94.6 %reduce-scatter.5.cloned.1.call-done = bf16[128,1024]{1,0:T(8,128)(2,1)} async-done(((bf16[1024,1024]{1,0:T(8,128)(2,1)}), bf16[128,1024]{1,0:T(8,128)(2,1)}) %reduce-scatter.5.cloned.1.call-update) | async-done | bytes 262160 | tf_op jit(solution)/shard_map/reduce_scatter | solution.py:31
Async XLA Ops:
  6.5 82.4 %all-gather.6.cloned.1.call-start = ((), (), s32[]{:S(2)}) async-start(), calls=%async_computation.2 | async-start | bytes 2359296 | tf_op jit(solution)/shard_map/all_gather | solution.py:8
  7.3 124.9 %all-gather.8.cloned.1.call-start = ((), (), s32[]{:S(2)}) async-start(), calls=%async_computation.3 | async-start | bytes 4587520 | tf_op jit(solution)/shard_map/all_gather | solution.py:10
  8.0 172.6 %all-gather.10.cloned.1.call-start = ((), (), s32[]{:S(2)}) async-start(), calls=%async_computation.4 | async-start | bytes 4587520 | tf_op jit(solution)/shard_map/all_gather | solution.py:11
  8.7 272.2 %reduce-scatter.3.cloned.1.call-start = ((), (), s32[]{:S(2)}) async-start(), calls=%async_computation.5 | async-start | bytes 8257536 | tf_op jit(solution)/shard_map/reduce_scatter | solution.py:15
  180.6 8.7 %copy-start = (bf16[1024,1792]{1,0:T(8,128)(2,1)S(1)}, bf16[1024,1792]{1,0:T(8,128)(2,1)}, u32[]{:S(2)}) copy-start(bf16[1024,1792]{1,0:T(8,128)(2,1)} %convolution_convert_fusion.1) | copy-start | bytes 11010052
  194.9 132.0 %all-gather.14.cloned.1.call-start = ((), (), s32[]{:S(2)}) async-start(), calls=%async_computation.7 | async-start | bytes 4587520 | tf_op jit(solution)/shard_map/all_gather | solution.py:28
  195.5 183.7 %all-gather.12.cloned.1.call-start = ((), (), s32[]{:S(2)}) async-start(), calls=%async_computation.6 | async-start | bytes 4128768 | tf_op jit(solution)/shard_map/all_gather | solution.py:25
  283.3 198.9 %reduce-scatter.5.cloned.1.call-start = ((), (), s32[]{:S(2)}) async-start(), calls=%async_computation.8 | async-start | bytes 2359296 | tf_op jit(solution)/shard_map/reduce_scatter | solution.py:31
Sparse Core Ops, SparseCore 0:
  10.0 78.8 all-gather.5
  90.7 41.3 all-gather.7
  133.9 46.6 all-gather.9
  195.0 85.8 reduce-scatter.2
  282.6 44.2 all-gather.13
  328.5 50.5 all-gather.11
  387.7 94.4 reduce-scatter.4
where the time goes:
time: 489 us
  waiting for transfers between devices  442 us (90%)
  matrix products  25.7 us (5%)
  between operations  13.5 us (3%)
  other arithmetic  7.89 us (2%)
    reduce_scatter x1, waiting for transfers between devices, on_device(): lax.psum_scatter(down_term.astype(jnp.bfloat16), 'col', scatter_dimension...  94.6 us
    reduce_scatter x1, waiting for transfers between devices, on_device(): lax.psum_scatter(jnp.concatenate((gate_term, up_term), axis=1).astype(jnp...  85.4 us
    all_gather x1, waiting for transfers between devices, on_device(): group_tokens = lax.all_gather(tokens, 'col', axis=0, tiled=True)  80.1 us
    all_gather x1, waiting for transfers between devices, on_device(): hidden_all = lax.all_gather(hidden, 'row', axis=0, tiled=True)  52.3 us
    all_gather x1, waiting for transfers between devices, on_device(): lax.all_gather(down_weight, 'dp', axis=0, tiled=True)  43.5 us
    all_gather x1, waiting for transfers between devices, on_device(): lax.all_gather(gate_weight, 'dp', axis=1, tiled=True)  43.2 us
    all_gather x1, waiting for transfers between devices, on_device(): lax.all_gather(up_weight, 'dp', axis=1, tiled=True)  40 us
  transfers between devices with their start and end apart: 7, of which 7 were waited for; matrix products, arithmetic and copies ran while one was open for 2% of the time, Pallas kernels for 0%

commit v1 on v0

--- a/solution.py
+++ b/solution.py
@@ -4,10 +4,20 @@
 from jax.sharding import PartitionSpec as P
 
 
+def work_the_ratios(unit, ax_name):
+    low = jnp.concatenate(
+        jax.lax.all_to_all(
+            jnp.stack([unit for _ in range(jax.lax.axis_size(ax_name))]), ax_name, 0, 0
+        ),
+        axis=1,
+    )
+    return low
+
+
 def on_device(tokens, gate_weight, up_weight, down_weight):
     group_tokens = lax.all_gather(tokens, "col", axis=0, tiled=True)
     gate_cols, up_cols = (
-        lax.all_gather(gate_weight, "dp", axis=1, tiled=True),
+        work_the_ratios(gate_weight, "dp"),
         lax.all_gather(up_weight, "dp", axis=1, tiled=True),
     )
     gate_term = jnp.dot(group_tokens, gate_cols, preferred_element_type=jnp.float32)

time: 489 us -> 441 us (0.902)
  waiting for transfers between devices: 442 us -> 345 us
  blocking collectives: 0 us -> 46.5 us
    all_gather x1, waiting for transfers between devices: 80.1 us -> 32.7 us  [on_device(): group_tokens = lax.all_gather(tokens, 'col', axis=0, tiled=True)]
    all_to_all x0 -> x1, blocking collectives: none -> 46.5 us  [work_the_ratios(): jax.lax.all_to_all(jnp.stack([unit for _ in range(jax.lax.axis_size(ax_na...]
    all_gather x1 -> x0, waiting for transfers between devices: 43.2 us -> none  [on_device(): lax.all_gather(gate_weight, 'dp', axis=1, tiled=True)]
    all_gather x1, waiting for transfers between devices: 40 us -> 34.7 us  [on_device(): lax.all_gather(up_weight, 'dp', axis=1, tiled=True)]
  transfers between devices with their start and end apart: 7 -> 6, of which waited for: 7 -> 6; matrix products, arithmetic and copies ran while one was open for 2% -> 3% of each run, Pallas kernels for 0% -> 0%
where the time goes in v1:
time: 441 us
  waiting for transfers between devices  345 us (78%)
  blocking collectives  46.5 us (11%)
  matrix products  25.7 us (6%)
  between operations  13.5 us (3%)
  other arithmetic  7.88 us (2%)
    reduce_scatter x1, waiting for transfers between devices, on_device(): lax.psum_scatter(down_term.astype(jnp.bfloat16), 'col', scatter_dimension...  94.7 us
    reduce_scatter x1, waiting for transfers between devices, on_device(): lax.psum_scatter(jnp.concatenate((gate_term, up_term), axis=1).astype(jnp...  85.4 us
    all_gather x1, waiting for transfers between devices, on_device(): hidden_all = lax.all_gather(hidden, 'row', axis=0, tiled=True)  52.3 us
    all_to_all x1, blocking collectives, work_the_ratios(): jax.lax.all_to_all(jnp.stack([unit for _ in range(jax.lax.axis_size(ax_na...  46.5 us
    all_gather x1, waiting for transfers between devices, on_device(): lax.all_gather(down_weight, 'dp', axis=0, tiled=True)  43.5 us
    all_gather x1, waiting for transfers between devices, on_device(): lax.all_gather(up_weight, 'dp', axis=1, tiled=True)  34.7 us
    all_gather x1, waiting for transfers between devices, on_device(): group_tokens = lax.all_gather(tokens, 'col', axis=0, tiled=True)  32.7 us
  transfers between devices with their start and end apart: 6, of which 6 were waited for; matrix products, arithmetic and copies ran while one was open for 3% of the time, Pallas kernels for 0%

profile of v1, /device:TPU:2, one launch (start us, length us, event | category | flops | bytes accessed | tf_op | source)
XLA Modules:
  0.0 440.6 jit_solution(13592587640558273527)
XLA Ops:
  6.5 0.0 all-gather.5.cloned.1.call-start
  6.5 0.7 all-gather.5.cloned.1.call-update
  7.3 0.0 all-gather.7.cloned.1.call-start
  7.3 0.7 all-gather.7.cloned.1.call-update
  8.0 0.0 reduce-scatter.3.cloned.1.call-start
  8.1 1.6 stack.2
  9.7 46.5 %all_to_all.5 = bf16[4,1024,448]{1,2,0:T(8,128)(2,1)} all-to-all(bf16[4,1024,448]{1,2,0:T(8,128)(2,1)S(1)} %stack.2), channel_id=1, replica_groups=mesh['dp'=4,'row'=8,'col'=8] {'dp'}, dimensions={0} | all-to-all | bytes 7340032 | tf_op jit(solution)/shard_map/all_to_all | solution.py:9
  56.2 32.7 %all-gather.5.cloned.1.call-done = bf16[1024,1024]{1,0:T(8,128)(2,1)} async-done(((bf16[128,1024]{1,0:T(8,128)(2,1)}), bf16[1024,1024]{1,0:T(8,128)(2,1)}) %all-gather.5.cloned.1.call-update) | async-done | bytes 2097168 | tf_op jit(solution)/shard_map/all_gather | solution.py:18
  88.9 8.5 %convolution_convert_fusion.1 = bf16[1024,1792]{1,0:T(8,128)(2,1)} fusion(bf16[1024,1024]{1,0:T(8,128)(2,1)} %all-gather.5.cloned.1.call-done, bf16[1024,1792]{0,1:T(8,128)(2,1)} %bitcast.9), kind=kOutput, calls=%fused_computation.2 | convolution fusion | flops 3759931392 | bytes 9437184 | tf_op jit(solution)/shard_map/dot_general | solution.py:23
  97.4 34.7 %all-gather.7.cloned.1.call-done = bf16[1024,1792]{0,1:T(8,128)(2,1)} async-done(((bf16[1024,448]{0,1:T(8,128)(2,1)}), bf16[1024,1792]{0,1:T(8,128)(2,1)}) %all-gather.7.cloned.1.call-update) | async-done | bytes 3670032 | tf_op jit(solution)/shard_map/all_gather | solution.py:21
  132.1 0.0 copy-start
  132.1 8.7 %convolution_convert_fusion = bf16[1024,1792]{1,0:T(8,128)(2,1)} fusion(bf16[1024,1024]{1,0:T(8,128)(2,1)} %all-gather.5.cloned.1.call-done, bf16[1024,1792]{0,1:T(8,128)(2,1)} %all-gather.7.cloned.1.call-done), kind=kOutput, calls=%fused_computation.1 | convolution fusion | flops 3759931392 | bytes 9437184 | tf_op jit(solution)/shard_map/dot_general | solution.py:24
  140.8 0.0 copy-done
  140.8 5.5 %pad_maximum_fusion = bf16[1024,3584]{1,0:T(8,128)(2,1)} fusion(bf16[1024,1792]{1,0:T(8,128)(2,1)} %convolution_convert_fusion, bf16[1024,1792]{1,0:T(8,128)(2,1)S(1)} %copy-done), kind=kLoop, calls=%fused_computation | loop fusion | flops 14680064 | bytes 14680064 | tf_op jit(solution)/shard_map/concatenate | solution.py:26
  146.3 0.0 reduce-scatter.3.cloned.1.call-update
  146.4 0.0 all-gather.11.cloned.1.call-start
  146.4 0.5 all-gather.11.cloned.1.call-update
  146.9 0.0 all-gather.9.cloned.1.call-start
  147.0 85.4 %reduce-scatter.3.cloned.1.call-done = bf16[128,3584]{1,0:T(8,128)(2,1)} async-done(((bf16[1024,3584]{1,0:T(8,128)(2,1)}), bf16[128,3584]{1,0:T(8,128)(2,1)}) %reduce-scatter.3.cloned.1.call-update) | async-done | bytes 917520 | tf_op jit(solution)/shard_map/reduce_scatter | solution.py:25
  232.4 1.4 convert_element_type.10
  233.8 1.0 fusion
  234.8 0.0 all-gather.9.cloned.1.call-update
  234.8 0.0 reduce-scatter.5.cloned.1.call-start
  234.9 43.5 %all-gather.11.cloned.1.call-done = bf16[1792,1024]{1,0:T(8,128)(2,1)} async-done(((bf16[448,1024]{1,0:T(8,128)(2,1)}), bf16[1792,1024]{1,0:T(8,128)(2,1)}) %all-gather.11.cloned.1.call-update) | async-done | bytes 3670032 | tf_op jit(solution)/shard_map/all_gather | solution.py:38
  278.4 52.3 %all-gather.9.cloned.1.call-done = bf16[1024,1792]{1,0:T(8,128)(2,1)} async-done(((bf16[128,1792]{1,0:T(8,128)(2,1)}), bf16[1024,1792]{1,0:T(8,128)(2,1)}) %all-gather.9.cloned.1.call-update) | async-done | bytes 3670032 | tf_op jit(solution)/shard_map/all_gather | solution.py:35
  330.6 8.4 %convolution_convert_fusion.2 = bf16[1024,1024]{1,0:T(8,128)(2,1)} fusion(bf16[1024,1792]{1,0:T(8,128)(2,1)} %all-gather.9.cloned.1.call-done, bf16[1792,1024]{1,0:T(8,128)(2,1)} %all-gather.11.cloned.1.call-done), kind=kOutput, calls=%fused_computation.3 | convolution fusion | flops 3759144960 | bytes 9437184 | tf_op jit(solution)/shard_map/dot_general | solution.py:36
  339.1 0.0 reduce-scatter.5.cloned.1.call-update
  339.1 94.7 %reduce-scatter.5.cloned.1.call-done = bf16[128,1024]{1,0:T(8,128)(2,1)} async-done(((bf16[1024,1024]{1,0:T(8,128)(2,1)}), bf16[128,1024]{1,0:T(8,128)(2,1)}) %reduce-scatter.5.cloned.1.call-update) | async-done | bytes 262160 | tf_op jit(solution)/shard_map/reduce_scatter | solution.py:41
Async XLA Ops:
  6.5 82.4 %all-gather.5.cloned.1.call-start = ((), (), s32[]{:S(2)}) async-start(), calls=%async_computation.3 | async-start | bytes 2359296 | tf_op jit(solution)/shard_map/all_gather | solution.py:18
  7.3 124.9 %all-gather.7.cloned.1.call-start = ((), (), s32[]{:S(2)}) async-start(), calls=%async_computation.4 | async-start | bytes 4587520 | tf_op jit(solution)/shard_map/all_gather | solution.py:21
  8.0 224.4 %reduce-scatter.3.cloned.1.call-start = ((), (), s32[]{:S(2)}) async-start(), calls=%async_computation.5 | async-start | bytes 8257536 | tf_op jit(solution)/shard_map/reduce_scatter | solution.py:25
  132.1 8.7 %copy-start = (bf16[1024,1792]{1,0:T(8,128)(2,1)S(1)}, bf16[1024,1792]{1,0:T(8,128)(2,1)}, u32[]{:S(2)}) copy-start(bf16[1024,1792]{1,0:T(8,128)(2,1)} %convolution_convert_fusion.1) | copy-start | bytes 11010052
  146.4 132.0 %all-gather.11.cloned.1.call-start = ((), (), s32[]{:S(2)}) async-start(), calls=%async_computation.7 | async-start | bytes 4587520 | tf_op jit(solution)/shard_map/all_gather | solution.py:38
  146.9 183.7 %all-gather.9.cloned.1.call-start = ((), (), s32[]{:S(2)}) async-start(), calls=%async_computation.6 | async-start | bytes 4128768 | tf_op jit(solution)/shard_map/all_gather | solution.py:35
  234.8 199.0 %reduce-scatter.5.cloned.1.call-start = ((), (), s32[]{:S(2)}) async-start(), calls=%async_computation.8 | async-start | bytes 2359296 | tf_op jit(solution)/shard_map/reduce_scatter | solution.py:41
Sparse Core Ops, SparseCore 0:
  10.0 78.8 all-gather.4
  90.7 41.3 all-gather.6
  146.5 85.8 reduce-scatter.2
  234.1 44.2 all-gather.10
  280.0 50.5 all-gather.8
  339.2 94.5 reduce-scatter.4
